TPU v7x, 32 devices: a whole 2x2x4 slice. The times are simulated.
32 devices in a mesh: row: 16 (over z, y, x), col: 2 (over core).
Axes of the slice: x: 2, y: 2, z: 4, core: 2. Of those that a mesh axis runs over, the one named last changes fastest.
Arguments:
- noise: bfloat16 [8, 2, 16, 2048], P(None, None, 'row', 'col'), may hold values from -6 to 6
- diag_factor: bfloat16 [2, 16, 2048, 2048], P(None, 'row', 'col'), may hold values from -0.125 to 0.125
- left_factor: bfloat16 [16, 32, 64, 2048], P('row', None, None, 'col'), may hold values from -0.125 to 0.125
- right_factor: bfloat16 [16, 32, 64, 2048], P('row', None, None, 'col'), may hold values from -0.125 to 0.125
- tile_ranks: int32 [16, 32], P('row'), may hold values from 1 to 64
- pair_first: int32 [16, 2, 4096], P('row', 'col'), may hold values from 4096 to 8191
- pair_partner: int32 [16, 2, 4096], P('row', 'col'), may hold values from 0 to 8191, as said below
- bin_ids: int32 [16, 2, 4096], P('row', 'col'), may hold values from 0 to 127, as said below
Outputs:
- samples: float32 [8, 2, 16, 2048], P(None, None, 'row', 'col')
- variogram: float32 [8, 128], replicated
Inputs may be any that keep to these rules, and one draw needn't show every extreme that they name: Pairs of the first tile-row pair (r = 0) have pair_partner of 4096 or more. `bin_ids`: bins may hold no pair.
All inputs are finite; a program needn't handle non-finite values.
Results may differ from a plain program's by a relative error of at most 0.0012.
Values may be sent and summed in bfloat16 or wider, within the bound.
A program may use at most 64 MiB of HBM per device.

v0:
```python
import jax
import jax.numpy as jnp
from jax import lax
from jax.sharding import PartitionSpec as P

NBIN = 128
PAIRS = 4096


def shifted(value, axis, steps):
    count = lax.axis_size(axis)
    leading, last = (max(0, -steps), min(count, count - steps))
    return lax.ppermute(value, axis, [(source, source + steps) for source in range(leading, last)])


def body(
    noise, diag_factor, left_factor, right_factor, tile_ranks, pair_first, pair_partner, bin_ids
):
    row_at = lax.axis_index("row")
    col_at = lax.axis_index("col")
    row_count = lax.axis_size("row")
    col_count = lax.axis_size("col")
    tile_count = 2 * row_count
    samples_n = noise.shape[0]
    shard_len = noise.shape[3]
    tile_len = shard_len * col_count
    columns = lax.all_gather(noise, "row", axis=2, tiled=True)
    segments = jnp.concatenate([columns[:, 0], columns[:, 1][:, ::-1]], axis=1)
    own_noise = lax.all_gather(noise, "col", axis=3, tiled=True)[:, :, 0]
    slot_ids = jnp.arange(tile_count, dtype=jnp.int32)
    source = jnp.where(slot_ids < row_at, slot_ids, slot_ids - row_at)
    chosen = jnp.take(segments, source, axis=1)
    partial_proj = jnp.einsum(
        "skt,kqt->ksq", chosen, right_factor[0], preferred_element_type=jnp.float32
    )
    projected = lax.psum(partial_proj, "col")
    rank_dim = right_factor.shape[2]
    in_rank = jnp.arange(rank_dim, dtype=jnp.int32)[None, :] < tile_ranks[0][:, None]
    coeffs = jnp.where(in_rank[:, None, :], projected, 0.0).astype(jnp.bfloat16)
    select = jnp.stack(
        [slot_ids < row_at, (slot_ids >= row_at) & (slot_ids < tile_count - 1)]
    ).astype(jnp.bfloat16)
    weighted = select[:, :, None, None] * coeffs[None]
    weighted = jnp.transpose(weighted, (0, 2, 1, 3)).reshape(2, samples_n, tile_count * rank_dim)
    factor_rows = left_factor[0].reshape(tile_count * rank_dim, shard_len)
    off_diag = jnp.einsum("hsm,mt->sht", weighted, factor_rows, preferred_element_type=jnp.float32)
    global_rows = col_at * shard_len + jnp.arange(shard_len, dtype=jnp.int32)
    col_ids = jnp.arange(tile_len, dtype=jnp.int32)
    tile_rows = diag_factor[:, 0]
    effective = jnp.where(
        col_ids[None, :] < global_rows[:, None], tile_rows, jnp.zeros((), jnp.bfloat16)
    )
    effective = effective + (col_ids[None, :] == global_rows[:, None]).astype(jnp.bfloat16)[None]
    on_diag = jnp.einsum("sht,hit->shi", own_noise, effective, preferred_element_type=jnp.float32)
    samples = (on_diag + off_diag)[:, :, None, :]
    own_tiles = lax.all_gather(samples, "col", axis=3, tiled=True)
    prev_tiles = shifted(own_tiles.astype(jnp.bfloat16), "row", 1).astype(own_tiles.dtype)
    pooled = jnp.concatenate(
        [prev_tiles[:, 0, 0], prev_tiles[:, 1, 0], own_tiles[:, 0, 0], own_tiles[:, 1, 0]], axis=1
    )
    first_idx = pair_first[0, 0]
    second_idx = pair_partner[0, 0]
    bin_local = bin_ids[0, 0]
    differ = jnp.take(pooled, first_idx, axis=1) - jnp.take(pooled, second_idx, axis=1)
    half_sq = 0.5 * differ * differ
    block_len = min(2048, PAIRS)
    bin_range = jnp.arange(NBIN, dtype=jnp.int32)
    bin_sums = jnp.zeros((samples_n, NBIN), jnp.float32)
    bin_counts = jnp.zeros((NBIN,), jnp.float32)
    for block_id in range(PAIRS // block_len):
        block_bins = bin_local[block_id * block_len : (block_id + 1) * block_len]
        onehot = (block_bins[:, None] == bin_range[None, :]).astype(jnp.float32)
        block_sq = half_sq[:, block_id * block_len : (block_id + 1) * block_len]
        bin_sums = bin_sums + jnp.dot(
            block_sq, onehot, precision=lax.Precision.HIGHEST, preferred_element_type=jnp.float32
        )
        bin_counts = bin_counts + jnp.sum(onehot, axis=0)
    totals, counts = lax.psum((bin_sums, bin_counts), ("row", "col"))
    variogram = totals / jnp.maximum(counts, 1.0)[None, :]
    return (samples, variogram)


def solution(mesh):
    in_specs = (
        P(None, None, "row", "col"),
        P(None, "row", "col", None),
        P("row", None, None, "col"),
        P("row", None, None, "col"),
        P("row", None),
        P("row", "col", None),
        P("row", "col", None),
        P("row", "col", None),
    )
    out_specs = (P(None, None, "row", "col"), P())
    return jax.shard_map(body, mesh=mesh, in_specs=in_specs, out_specs=out_specs, check_vma=False)
```

profile of v0, /device:TPU:0, one launch (start us, length us, event | category | flops | bytes accessed | tf_op | source)
XLA Modules:
  0.0 148.2 jit_solution(3727056075110280351)
XLA Ops:
  0.7 0.8 copy.29
  1.4 0.8 copy.28
  2.2 45.3 %all_gather.10 = bf16[8,2,16,1024]{3,0,2,1:T(8,128)(2,1)S(1)} all-gather(bf16[8,2,1,1024]{3,0,2,1:T(8,128)(2,1)S(1)} %copy.29), channel_id=1, replica_groups=mesh['row'=16,'col'=2] {'row'}, dimensions={2}, use_global_device_ids=true | all-gather | bytes 557056 | tf_op jit(solution)/shard_map/all_gather | solution.py:27
  47.7 0.6 gather_fusion
  48.3 3.4 %fusion.5 = f32[32,8,64]{2,1,0:T(8,128)S(1)} fusion(bf16[1,32,64,1024]{3,2,1,0:T(8,128)(2,1)} %param.13, bf16[32,8,1024]{2,1,0:T(8,128)(2,1)S(1)} %gather_fusion, pred[32]{0:T(512)(128)(4,1)S(1)} %compare_and_fusion.2), kind=kOutput, calls=%fused_computation.10 | convolution fusion | flops 33816576 | bytes 4784160 | tf_op jit(solution)/shard_map/skt,kqt->ksq/dot_general | solution.py:33
  51.7 3.9 %psum.21 = bf16[32,8,64]{2,1,0:T(8,128)(2,1)S(1)} all-reduce(f32[32,8,64]{2,1,0:T(8,128)S(1)} %fusion.5), channel_id=1, replica_groups=mesh['row'=16,'col'=2] {'col'}, use_global_device_ids=true, to_apply=%region_0.1 | all-reduce | flops 16384 | bytes 98304 | tf_op jit(solution)/shard_map/psum | solution.py:36
  55.6 0.0 copy-done.4
  55.6 0.1 iota_compare_fusion.6
  55.7 0.1 mul.40
  55.9 0.1 mul.36
  55.9 0.1 mul.37
  56.0 3.6 %fusion.3 = (bf16[1024,2048]{1,0:T(8,128)(2,1)S(1)}, pred[1024,2048]{1,0:T(8,128)(4,1)S(1)}) fusion(s32[1024]{0:T(1024)S(1)} %iota_add_fusion), kind=kLoop, calls=%fused_computation.8 | loop fusion | flops 6291456 | bytes 6295552 | tf_op jit(solution)/shard_map/convert_element_type | solution.py:53
  59.7 1.9 %all_gather.9 = bf16[8,2,1,2048]{3,0,1,2:T(8,128)(2,1)S(1)} all-gather(bf16[8,2,1,1024]{3,0,1,2:T(8,128)(2,1)S(1)} %copy.28), channel_id=1, replica_groups=mesh['row'=16,'col'=2] {'col'}, dimensions={3}, use_global_device_ids=true | all-gather | bytes 98304 | tf_op jit(solution)/shard_map/all_gather | solution.py:29
  61.5 4.9 %fusion.9 = f32[8,2,1024]{2,0,1:T(8,128)S(1)} fusion(bf16[2,1,1024,2048]{3,2,1,0:T(8,128)(2,1)} %param.11, pred[1024,2048]{1,0:T(8,128)(4,1)S(1)} %get-tuple-element.18, bf16[1024,2048]{1,0:T(8,128)(2,1)S(1)} %get-tuple-element.17, bf16[8,2,1,2048]{3,0,1,2:T(8,128)(2,1)S(1)} %all_gather.9), kind=kOutput, calls=%fused_computation.16 | convolution fusion | flops 75497472 | bytes 14811136 | tf_op jit(solution)/shard_map/sht,hit->shi/dot_general | solution.py:54
  66.4 0.0 copy-start.3
  66.5 0.0 copy-done
  66.5 0.7 fusion.12
  67.1 1.9 %all-gather = f32[8,2,2048]{2,0,1:T(8,128)S(1)} all-gather(f32[8,2,1024]{2,0,1:T(8,128)S(1)} %fusion.12), channel_id=2, replica_groups=mesh['row'=16,'col'=2] {'col'}, dimensions={2}, use_global_device_ids=true | all-gather | bytes 196608 | tf_op jit(solution)/shard_map/all_gather | solution.py:56
  69.0 1.3 collective-permute-start
  70.3 0.0 copy-done.2
  70.4 0.0 copy-done.1
  70.4 1.2 convert_reduce_fusion
  71.7 0.7 copy.37
  72.4 0.1 collective-permute-done
  72.5 2.6 %copy.35 = f32[8,8192]{0,1:T(8,128)} copy(f32[8,8192]{1,0:T(8,128)S(1)} %pad_maximum_fusion.1) | data formatting | bytes 524288 | tf_op jit(solution)/shard_map/concatenate | solution.py:58
  75.1 13.0 %gather_fusion.1 = f32[4096,8]{1,0:T(8,128)S(1)} fusion(f32[8,8192]{0,1:T(8,128)} %copy.35, s32[4096]{0:T(1024)S(1)} %fusion.27), kind=kCustom, calls=%fused_computation.clone | custom fusion | bytes 278528 | tf_op jit(solution)/shard_map/jit(_take)/gather | solution.py:64
  88.1 16.4 %gather_fusion.2 = f32[4096,8]{1,0:T(8,128)} fusion(f32[8,8192]{0,1:T(8,128)} %copy.35, s32[4096]{0:T(1024)S(1)} %fusion.28), kind=kCustom, calls=%fused_computation.1.clone | custom fusion | bytes 278528 | tf_op jit(solution)/shard_map/jit(_take)/gather | solution.py:64
  104.5 3.2 %multiply_multiply_fusion = f32[8,4096]{0,1:T(8,128)S(1)} fusion(f32[4096,8]{1,0:T(8,128)} %gather_fusion.2, f32[4096,8]{1,0:T(8,128)S(1)} %gather_fusion.1, pred[4096]{0:T(1024)(128)(4,1)S(1)} %get-tuple-element.21, pred[4096]{0:T(1024)(128)(4,1)S(1)} %get-tuple-element.22), kind=kLoop, calls=%fused_computation.14 | loop fusion | flops 163840 | bytes 401408 | tf_op jit(solution)/shard_map/mul | solution.py:65
  107.7 1.2 fusion.14
  108.9 1.3 convolution_add_fusion
  110.1 37.5 %all-reduce = (f32[8,128]{1,0:T(8,128)S(1)}, f32[128]{0:T(128)S(1)}) all-reduce(f32[8,128]{1,0:T(8,128)S(1)} %convolution_add_fusion, f32[128]{0:T(128)S(1)} %add.70), channel_id=1, replica_groups=mesh['row'=16,'col'=2] {'row','col'}, use_global_device_ids=true, to_apply=%region_1.3 | all-reduce | flops 1152 | bytes 9216 | tf_op jit(solution)/shard_map/psum | solution.py:78
  147.6 0.6 broadcast_divide_fusion
  (28 shorter events, 0.3 us)
Async XLA Ops:
  47.5 8.0 %copy-start.4 = (s32[1,32]{1,0:T(1,128)S(1)}, s32[1,32]{1,0:T(1,128)}, u32[]{:S(2)}) copy-start(s32[1,32]{1,0:T(1,128)} %param.14) | copy-start | bytes 388
  61.5 4.9 %copy-start = (bf16[1,32,64,1024]{3,2,1,0:T(8,128)(2,1)S(1)}, bf16[1,32,64,1024]{3,2,1,0:T(8,128)(2,1)}, u32[]{:S(2)}) copy-start(bf16[1,32,64,1024]{3,2,1,0:T(8,128)(2,1)} %param.12) | copy-start | bytes 12582916
  66.4 3.9 %copy-start.2 = (s32[1,1,4096]{2,1,0:T(1,128)S(1)}, s32[1,1,4096]{2,1,0:T(1,128)}, u32[]{:S(2)}) copy-start(s32[1,1,4096]{2,1,0:T(1,128)} %param.15) | copy-start | bytes 49156
  66.4 3.9 %copy-start.1 = (s32[1,1,4096]{2,1,0:T(1,128)S(1)}, s32[1,1,4096]{2,1,0:T(1,128)}, u32[]{:S(2)}) copy-start(s32[1,1,4096]{2,1,0:T(1,128)} %param.16) | copy-start | bytes 49156
  66.4 4.0 %copy-start.3 = (s32[1,1,4096]{2,1,0:T(1,128)S(1)}, s32[1,1,4096]{2,1,0:T(1,128)}, u32[]{:S(2)}) copy-start(s32[1,1,4096]{2,1,0:T(1,128)} %param.17) | copy-start | bytes 49156
  69.0 3.4 %collective-permute-start = (bf16[8,2,1,2048]{3,0,2,1:T(8,128)(2,1)S(1)}, bf16[8,2,1,2048]{3,0,2,1:T(8,128)(2,1)S(1)}, u32[]{:S(2)}, u32[]{:S(2)}) collective-permute-start(bf16[8,2,1,2048]{3,0,2,1:T(8,128)(2,1)S(1)} %bitcast_convert_fusion), channel_id=1, source_target_pairs={{0,2},{2,4},{4,6},{6,8},{8,10},{10,12},{12,14},{14,16},{16,18},{18... | collective-permute-start | bytes 196616 | tf_op jit(solution)/shard_map/ppermute | solution.py:13
where the time goes:
time: 150 us; the launch traced here: 148 us
  blocking collectives  90.4 us (60%)
  local copies, waits for them, and re-layouts  35.2 us (23%)
  matrix products  11.5 us (8%)
  other arithmetic  8.9 us (6%)
    all_gather x1, blocking collectives, body(): columns = lax.all_gather(noise, 'row', axis=2, tiled=True)  45.3 us
    psum x1, blocking collectives, body(): totals, counts = lax.psum((bin_sums, bin_counts), ('row', 'col'))  37.5 us
    gather x1, local copies, waits for them, and re-layouts, body(): jnp.take(pooled, second_idx, axis=1)  16.4 us
    gather x1, local copies, waits for them, and re-layouts, body(): jnp.take(pooled, first_idx, axis=1) - jnp.take(pooled, second_idx, axis=1)  13 us
    dot_general x1, matrix products, body(): jnp.einsum('sht,hit->shi', own_noise, effective, preferred_element_type=j...  4.92 us
    psum x1, blocking collectives, body(): projected = lax.psum(partial_proj, 'col')  3.85 us
    convert_element_type x1, other arithmetic, body(): (col_ids[None, :] == global_rows[:, None]).astype(jnp.bfloat16)[None]  3.63 us
    dot_general x1, matrix products, body(): jnp.einsum('skt,kqt->ksq', chosen, right_factor[0], preferred_element_typ...  3.45 us
  transfers between devices with their start and end apart: 1, of which 1 were waited for; matrix products, arithmetic and copies ran while one was open for 1% of the time, Pallas kernels for 0%

commit v1 on v0

v1 whole, which is shorter than its diff:
```python
import functools

import jax
import jax.numpy as jnp
from jax import lax
from jax.experimental import pallas as pl
from jax.experimental.pallas import tpu as pltpu
from jax.sharding import PartitionSpec as P

NBIN = 128
LANES = 128
PLANE = 4
MESH = pl.DeviceIdType.MESH
NT_DIMS = (((1,), (1,)), ((), ()))


def kernel(
    dims,
    z_ref, diag_ref, left_ref, right_ref, ranks_ref, first_ref, second_ref, bins_ref,
    samples_ref, vario_ref,
    zbuf, zpeer, down, doff, vbuf, ubuf, proj, acc, full, sbf, prev, prev32, diff, red1, red2, red3,
    own_sem, off_sem, v_sem, u_sem,
    z_send, z_recv, zp_send, zp_recv, pj_send, pj_recv, sm_send, sm_recv, pv_send, pv_recv,
    r1_send, r1_recv, r2_send, r2_recv, r3_send, r3_recv,
):
    rows, cols, count, shard, tile, rank, strip = dims
    layers = rows // PLANE
    tiles = 2 * rows
    r = lax.axis_index("row")
    c = lax.axis_index("col")
    b = lax.rem(r, PLANE)
    a = lax.div(r, PLANE)
    x_at = lax.rem(r, 2)
    y_at = lax.div(b, 2)
    x_step = 1 - 2 * x_at
    y_step = 2 - 4 * y_at
    strips = shard // strip
    pending = []

    def remote(src, dst, send, recv, row, col):
        return pltpu.make_async_remote_copy(
            src_ref=src, dst_ref=dst, send_sem=send, recv_sem=recv,
            device_id=(row, col), device_id_type=MESH,
        )

    def push(*args):
        copy = remote(*args)
        copy.start()
        pending.append(copy)

    own_copies = {}
    off_copies = {}
    for h in range(2):
        for s in range(strips):
            width = (s + 1) * strip
            own_copies[h, s] = pltpu.make_async_copy(
                diag_ref.at[h, pl.ds(s * strip, strip), pl.ds(pl.multiple_of(c * shard, LANES), width)],
                down.at[h, pl.ds(s * strip, strip), pl.ds(0, width)],
                own_sem.at[h, s],
            )
            own_copies[h, s].start()
    for h in range(2):
        for d in range(1, cols):
            at = jnp.maximum(c - d, 0)
            off_copies[h, d] = pltpu.make_async_copy(
                diag_ref.at[h, :, pl.ds(pl.multiple_of(at * shard, LANES), shard)],
                doff.at[h, d - 1],
                off_sem.at[h, d - 1],
            )

            @pl.when(c >= d)
            def _(copy=off_copies[h, d]):
                copy.start()

    v_parts = v_sem.shape[0]
    part = tiles * rank // v_parts
    v_copies = [
        pltpu.make_async_copy(right_ref.at[pl.ds(i * part, part)], vbuf.at[pl.ds(i * part, part)], v_sem.at[i])
        for i in range(v_parts)
    ]
    u_copies = [
        pltpu.make_async_copy(left_ref.at[pl.ds(i * part, part)], ubuf.at[pl.ds(i * part, part)], u_sem.at[i])
        for i in range(v_parts)
    ]
    for copy in v_copies + u_copies:
        copy.start()

    barrier = pltpu.get_barrier_semaphore()

    def greet(row, col):
        pl.semaphore_signal(barrier, inc=1, device_id=(row, col), device_id_type=MESH)

    col_peers = [lax.rem(c + d, cols) for d in range(1, cols)]
    plane_peers = [a * PLANE + lax.rem(b + d, PLANE) for d in range(1, PLANE)]
    layer_peers = [lax.rem(a + d, layers) * PLANE + b for d in range(1, layers)]
    for peer in layer_peers + plane_peers:
        greet(peer, c)
    for peer in col_peers:
        greet(r, peer)

    @pl.when(r < rows - 1)
    def _():
        for k in range(cols):
            greet(r + 1, k)

    @pl.when(r > 0)
    def _():
        for k in range(cols):
            greet(r - 1, k)

    expected = (cols - 1) + (PLANE - 1) + (layers - 1)
    expected = expected + jnp.where(r < rows - 1, cols, 0) + jnp.where(r > 0, cols, 0)
    pl.semaphore_wait(barrier, expected)

    def tile_of(owner, h):
        return owner if h == 0 else tiles - 1 - owner

    send_at = [0]

    def z_push(src, owner, h, row):
        j = tile_of(owner, h)
        push(src, zbuf.at[j], z_send.at[send_at[0]], z_recv.at[j], row, c)
        send_at[0] += 1

    def z_wait(owner, h):
        j = tile_of(owner, h)
        remote(zbuf.at[j], zbuf.at[j], z_send.at[0], z_recv.at[j], r, c).wait_recv()

    row_x = r + x_step
    row_y = r + y_step
    near = (row_y, row_x)
    far = (row_x, row_y)
    for peer in layer_peers:
        for h in range(2):
            z_push(z_ref.at[h], r, h, peer)
    for h in range(2):
        z_push(z_ref.at[h], r, h, near[h])
        z_push(z_ref.at[h], r, h, far[h])
    for i, peer in enumerate(col_peers):
        push(z_ref, zpeer.at[c], zp_send.at[i], zp_recv.at[c], r, peer)
    for h in range(2):
        zbuf[tile_of(r, h)] = z_ref[h]

    def diag_chunk(h, s):
        own_copies[h, s].wait()
        lanes = pl.ds(s * strip, strip)
        block = down[h, lanes, lanes]
        below = (
            lax.broadcasted_iota(jnp.int32, (strip, strip), 1)
            < lax.broadcasted_iota(jnp.int32, (strip, strip), 0)
        )
        block = jnp.where(below, block.astype(jnp.float32), 0.0).astype(jnp.bfloat16)
        mine = z_ref[h, :, lanes]
        value = mine.astype(jnp.float32)
        value += lax.dot_general(mine, block, NT_DIMS, preferred_element_type=jnp.float32)
        if s:
            value += lax.dot_general(
                z_ref[h, :, : s * strip], down[h, lanes, : s * strip], NT_DIMS,
                preferred_element_type=jnp.float32,
            )
        acc[h * count : (h + 1) * count, lanes] = value

    def off_chunk(h, d):
        @pl.when(c >= d)
        def _():
            off_copies[h, d].wait()
            at = jnp.maximum(c - d, 0)
            acc[h * count : (h + 1) * count, :] += lax.dot_general(
                zpeer[at, h], doff[h, d - 1], NT_DIMS, preferred_element_type=jnp.float32
            )

    work = [functools.partial(diag_chunk, h, s) for h in range(2) for s in range(strips)]
    spare = [functools.partial(off_chunk, h, d) for h in range(2) for d in range(1, cols)]

    def some(n):
        for _ in range(n):
            if work:
                work.pop(0)()

    some(strips)
    layer_owner = [lax.rem(a + d, layers) * PLANE + b for d in range(1, layers)]
    for owner in layer_owner:
        for h in range(2):
            z_wait(owner, h)
            j = tile_of(owner, h)
            z_push(zbuf.at[j], owner, h, near[h])
            z_push(zbuf.at[j], owner, h, far[h])
        some(1)
    some(len(work))
    for i, peer in enumerate(col_peers):
        remote(z_ref, zpeer.at[peer], zp_send.at[i], zp_recv.at[peer], r, peer).wait_recv()
    second_step = (y_step, x_step)
    for owner in [r] + layer_owner:
        for h in range(2):
            from_near = owner + second_step[h]
            z_wait(from_near, h)
            j = tile_of(from_near, h)
            z_push(zbuf.at[j], from_near, h, far[h])
        if spare:
            spare.pop(0)()
    while spare:
        spare.pop(0)()
    last_step = (x_step, y_step)
    for owner in [r] + layer_owner:
        for h in range(2):
            z_wait(owner + last_step[h], h)
            z_wait(owner + x_step + y_step, h)

    group = 256 // rank
    lane_slot = lax.div(lax.broadcasted_iota(jnp.int32, (count, group * rank), 1), rank)
    lane_rank = lax.rem(lax.broadcasted_iota(jnp.int32, (count, group * rank), 1), rank)
    waited = 0
    for g in range(tiles // group):
        while waited * part < (g + 1) * group * rank:
            v_copies[waited].wait()
            waited += 1
        chosen = []
        for i in range(group):
            k = g * group + i
            chosen.append(zbuf[jnp.where(k < r, k, jnp.maximum(k - r, 0))].astype(jnp.float32))
        lhs = jnp.concatenate(chosen, axis=0).astype(jnp.bfloat16)
        span = pl.ds(g * group * rank, group * rank)
        result = lax.dot_general(lhs, vbuf[span, :], NT_DIMS, preferred_element_type=jnp.float32)
        value = result[:count]
        for i in range(1, group):
            value = jnp.where(lane_slot == i, result[i * count : (i + 1) * count], value)
        proj[c, :, span] = value
    for i, peer in enumerate(col_peers):
        push(proj.at[c], proj.at[c], pj_send.at[i], pj_recv.at[c], r, peer)
    for copy in u_copies:
        copy.wait()
    for i, peer in enumerate(col_peers):
        remote(proj.at[c], proj.at[peer], pj_send.at[i], pj_recv.at[peer], r, peer).wait_recv()
    weighted = []
    for g in range(tiles // group):
        span = pl.ds(g * group * rank, group * rank)
        value = proj[0, :, span]
        for k in range(1, cols):
            value = value + proj[k, :, span]
        limit = jnp.zeros((count, group * rank), jnp.int32)
        for i in range(group):
            limit = jnp.where(lane_slot == i, ranks_ref[0, g * group + i], limit)
        value = jnp.where(lane_rank < limit, value, 0.0)
        slot = lane_slot + g * group
        weighted.append(
            jnp.concatenate(
                [
                    jnp.where(slot < r, value, 0.0),
                    jnp.where((slot >= r) & (slot < tiles - 1), value, 0.0),
                ],
                axis=0,
            ).astype(jnp.bfloat16)
        )
    weights = jnp.concatenate(weighted, axis=1)
    value = acc[...] + jnp.dot(weights, ubuf[...], preferred_element_type=jnp.float32)
    full[c] = value
    sbf[...] = value.astype(jnp.bfloat16)
    for i, peer in enumerate(col_peers):
        push(full.at[c], full.at[c], sm_send.at[i], sm_recv.at[c], r, peer)
    prev_copies = [
        remote(sbf, prev.at[c], pv_send.at[k], pv_recv.at[c], jnp.minimum(r + 1, rows - 1), k)
        for k in range(cols)
    ]

    @pl.when(r < rows - 1)
    def _():
        for copy in prev_copies:
            copy.start()

    for h in range(2):
        samples_ref[h] = value[h * count : (h + 1) * count]
    for i, peer in enumerate(col_peers):
        remote(full.at[c], full.at[peer], sm_send.at[i], sm_recv.at[peer], r, peer).wait_recv()

    groups = first_ref.shape[0]
    per_row = shard // LANES
    own_first = 2 * tile // LANES
    batch = 4

    def table(ref, h, j):
        return ref[j // per_row, h * count : (h + 1) * count, (j % per_row) * LANES : (j % per_row + 1) * LANES]

    def split(ref, at):
        index = jnp.broadcast_to(ref[pl.ds(at, 1), :], (count, LANES))
        return lax.shift_right_logical(index, 7), lax.bitwise_and(index, LANES - 1)

    def pick(entry, low):
        return jnp.take_along_axis(entry, low, axis=1, mode="promise_in_bounds")

    def own_part(step, carry):
        ats = [step * batch + i for i in range(batch)]
        one = [split(first_ref, at) for at in ats]
        two = [split(second_ref, at) for at in ats]
        got_one = [jnp.zeros((count, LANES), jnp.float32) for _ in ats]
        got_two = [jnp.zeros((count, LANES), jnp.float32) for _ in ats]
        for h in range(2):
            for j in range(tile // LANES):
                entry = table(full, h, j)
                number = own_first + h * (tile // LANES) + j
                for i in range(batch):
                    got_one[i] = jnp.where(one[i][0] == number, pick(entry, one[i][1]), got_one[i])
                    got_two[i] = jnp.where(two[i][0] == number, pick(entry, two[i][1]), got_two[i])
        for i in range(batch):
            diff[ats[i]] = got_one[i] - got_two[i]
        return carry

    lax.fori_loop(0, groups // batch, own_part, 0)

    @pl.when(r > 0)
    def _():
        for k in range(cols):
            remote(sbf, prev.at[k], pv_send.at[k], pv_recv.at[k], r, c).wait_recv()
        prev32[...] = prev[...].astype(jnp.float32)

    @pl.when(r == 0)
    def _():
        prev32[...] = jnp.zeros_like(prev32)

    bin_rows = lax.broadcasted_iota(jnp.int32, (NBIN, LANES), 0)

    def prev_part(step, sums):
        ats = [step * batch + i for i in range(batch)]
        two = [split(second_ref, at) for at in ats]
        got = [jnp.zeros((count, LANES), jnp.float32) for _ in ats]
        for h in range(2):
            for j in range(tile // LANES):
                entry = table(prev32, h, j)
                number = h * (tile // LANES) + j
                for i in range(batch):
                    got[i] = jnp.where(two[i][0] == number, pick(entry, two[i][1]), got[i])
        for i in range(batch):
            differ = diff[ats[i]] - got[i]
            half_sq = 0.5 * differ * differ
            high = half_sq.astype(jnp.bfloat16).astype(jnp.float32)
            terms = jnp.concatenate(
                [high, half_sq - high, jnp.ones((count, LANES), jnp.float32)], axis=0
            ).astype(jnp.bfloat16)
            onehot = jnp.where(
                jnp.broadcast_to(bins_ref[pl.ds(ats[i], 1), :], (NBIN, LANES)) == bin_rows, 1.0, 0.0
            ).astype(jnp.bfloat16)
            sums = sums + lax.dot_general(terms, onehot, NT_DIMS, preferred_element_type=jnp.float32)
        return sums

    sums = lax.fori_loop(0, groups // batch, prev_part, jnp.zeros((3 * count, NBIN), jnp.float32))
    total = jnp.concatenate([sums[:count] + sums[count : 2 * count], sums[2 * count :]], axis=0)

    def reduce_stage(value, buf, at, peers, send, recv, number):
        buf[at] = value
        for i, (row, col, slot) in enumerate(peers):
            push(buf.at[at], buf.at[at], send.at[i], recv.at[at], row, col)
        for i, (row, col, slot) in enumerate(peers):
            remote(buf.at[at], buf.at[slot], send.at[i], recv.at[slot], row, col).wait_recv()
        out = buf[0]
        for i in range(1, number):
            out = out + buf[i]
        return out

    total = reduce_stage(total, red1, c, [(r, p, p) for p in col_peers], r1_send, r1_recv, cols)
    total = reduce_stage(
        total, red2, b, [(p, c, lax.rem(p, PLANE)) for p in plane_peers], r2_send, r2_recv, PLANE
    )
    total = reduce_stage(
        total, red3, a, [(p, c, lax.div(p, PLANE)) for p in layer_peers], r3_send, r3_recv, layers
    )
    vario_ref[...] = total[:count] / jnp.maximum(total[count:], 1.0)

    for copy in pending:
        copy.wait_send()

    @pl.when(r < rows - 1)
    def _():
        for copy in prev_copies:
            copy.wait_send()


def body(
    noise, diag_factor, left_factor, right_factor, tile_ranks, pair_first, pair_partner, bin_ids
):
    rows = lax.axis_size("row")
    cols = lax.axis_size("col")
    count = noise.shape[0]
    shard = noise.shape[3]
    tile = shard * cols
    tiles = 2 * rows
    rank = right_factor.shape[2]
    strip = min(256, shard)
    layers = rows // PLANE
    v_parts = 4
    z = jnp.transpose(noise[:, :, 0], (1, 0, 2))
    dma = lambda *shape: pltpu.SemaphoreType.DMA(shape)
    vmem = pl.BlockSpec(memory_space=pltpu.VMEM)
    hbm = pl.BlockSpec(memory_space=pl.ANY)
    smem = pl.BlockSpec(memory_space=pltpu.SMEM)
    off = max(cols - 1, 1)
    f32, bf16 = jnp.float32, jnp.bfloat16
    samples, vario = pl.pallas_call(
        functools.partial(kernel, (rows, cols, count, shard, tile, rank, strip)),
        out_shape=(
            jax.ShapeDtypeStruct((2, count, shard), f32),
            jax.ShapeDtypeStruct((count, NBIN), f32),
        ),
        in_specs=[vmem, hbm, hbm, hbm, smem, vmem, vmem, vmem],
        out_specs=(vmem, vmem),
        scratch_shapes=[
            pltpu.VMEM((tiles, count, shard), bf16),
            pltpu.VMEM((cols, 2, count, shard), bf16),
            pltpu.VMEM((2, shard, shard), bf16),
            pltpu.VMEM((2, off, shard, shard), bf16),
            pltpu.VMEM((tiles * rank, shard), bf16),
            pltpu.VMEM((tiles * rank, shard), bf16),
            pltpu.VMEM((cols, count, tiles * rank), f32),
            pltpu.VMEM((2 * count, shard), f32),
            pltpu.VMEM((cols, 2 * count, shard), f32),
            pltpu.VMEM((2 * count, shard), bf16),
            pltpu.VMEM((cols, 2 * count, shard), bf16),
            pltpu.VMEM((cols, 2 * count, shard), f32),
            pltpu.VMEM((pair_first.shape[2] // LANES, count, LANES), f32),
            pltpu.VMEM((cols, 2 * count, NBIN), f32),
            pltpu.VMEM((PLANE, 2 * count, NBIN), f32),
            pltpu.VMEM((layers, 2 * count, NBIN), f32),
            dma(2, shard // strip), dma(2, off), dma(v_parts), dma(v_parts),
            dma(2 * (layers - 1) + 6 * layers + 8), dma(tiles), dma(off), dma(cols),
            dma(off), dma(cols), dma(off), dma(cols), dma(cols), dma(cols),
            dma(off), dma(cols), dma(PLANE), dma(PLANE), dma(layers), dma(layers),
        ],
        compiler_params=pltpu.CompilerParams(collective_id=0, has_side_effects=True),
    )(
        z,
        diag_factor.reshape(2, shard, tile),
        left_factor.reshape(tiles * rank, shard),
        right_factor.reshape(tiles * rank, shard),
        tile_ranks,
        pair_first.reshape(-1, LANES),
        pair_partner.reshape(-1, LANES),
        bin_ids.reshape(-1, LANES),
    )
    return jnp.transpose(samples, (1, 0, 2))[:, :, None, :], vario


def solution(mesh):
    in_specs = (
        P(None, None, "row", "col"),
        P(None, "row", "col", None),
        P("row", None, None, "col"),
        P("row", None, None, "col"),
        P("row", None),
        P("row", "col", None),
        P("row", "col", None),
        P("row", "col", None),
    )
    out_specs = (P(None, None, "row", "col"), P())
    return jax.shard_map(body, mesh=mesh, in_specs=in_specs, out_specs=out_specs, check_vma=False)
```

time: 150 us -> 46 us (0.31)
  blocking collectives: 90.4 us -> 0 us
  Pallas kernels: 0 us -> 40.8 us
  local copies, waits for them, and re-layouts: 35.2 us -> 4.19 us
  matrix products: 11.5 us -> 0 us
  other arithmetic: 8.9 us -> 0 us
    all_gather x3 -> x0, blocking collectives: 49.1 us -> none  [the longest x1 45.3 us: body(): columns = lax.all_gather(noise, 'row', axis=2, tiled=True)]
    psum x2 -> x0, blocking collectives: 41.3 us -> none  [the longest x1 37.5 us: body(): totals, counts = lax.psum((bin_sums, bin_counts), ('row', 'col'))]
    pallas_call x0 -> x1, Pallas kernels: none -> 40.8 us  [body(): pl.pallas_call(functools.partial(kernel, (rows, cols, count, shard, tile,...]
    gather x3 -> x0, local copies, waits for them, and re-layouts: 29.9 us -> none  [the longest x1 16.4 us: body(): jnp.take(pooled, second_idx, axis=1)]
    dot_general x5 -> x0, matrix products: 11.5 us -> none  [the longest x1 4.92 us: body(): jnp.einsum('sht,hit->shi', own_noise, effective, preferred_element_type=j...]
    convert_element_type x4 -> x0, other arithmetic: 3.66 us -> none  [the longest x1 3.63 us: body(): (col_ids[None, :] == global_rows[:, None]).astype(jnp.bfloat16)[None]]
    mul x2 -> x0, other arithmetic: 3.21 us -> none  [the longest x1 3.18 us: body(): half_sq = 0.5 * differ * differ]
    concatenate x1 -> x0, local copies, waits for them, and re-layouts: 2.59 us -> none  [body(): jnp.concatenate([prev_tiles[:, 0, 0], prev_tiles[:, 1, 0], own_tiles[:, 0...]
  transfers between devices with their start and end apart: 1 -> 0, of which waited for: 1 -> 0; matrix products, arithmetic and copies ran while one was open for 1% -> 0% of each run, Pallas kernels for 0% -> 0%
where the time goes in v1:
time: 46 us; the launch traced here: 45.6 us
  Pallas kernels  40.8 us (89%)
  local copies, waits for them, and re-layouts  4.19 us (9%)
  between operations  0.64 us (1%)
    pallas_call x1, Pallas kernels, body(): pl.pallas_call(functools.partial(kernel, (rows, cols, count, shard, tile,...  40.8 us
    unnamed x3, local copies, waits for them, and re-layouts  4.19 us

profile of v1, /device:TPU:0, one launch (start us, length us, event | category | flops | bytes accessed | tf_op | source)
XLA Modules:
  0.0 45.6 jit_solution(15997564333685769181)
XLA Ops:
  0.6 1.4 %copy.13 = bf16[8,2,1,1024]{3,0,1,2:T(8,128)(2,1)} copy(bf16[8,2,1,1024]{3,1,2,0:T(2,128)(2,1)} %param.8) | data formatting | bytes 65536 | tf_op args[0]
  2.0 40.8 %shard_map.95 = (f32[2,8,1024]{2,1,0:T(8,128)}, f32[8,128]{1,0:T(8,128)}) custom-call(bf16[2,8,1024]{2,1,0:T(8,128)(2,1)} %bitcast.17, bf16[2,1024,2048]{2,1,0:T(8,128)(2,1)} %bitcast.14, bf16[2048,1024]{1,0:T(8,128)(2,1)} %bitcast.15, bf16[2048,1024]{1,0:T(8,128)(2,1)} %bitcast.16, s32[1,32]{1,0:T(1,128)} %ranks_ref.1, s32[32,128]{1,0:T(8,128)} %bitcast.19, ...), custom_call_target="tpu_custom_call" | custom-call | tf_op jit(solution)/shard_map/pallas_call | solution.py:396
  42.8 1.5 %copy.11 = f32[8,2,1,1024]{3,2,1,0:T(1,128)} copy(f32[8,2,1,1024]{3,0,1,2:T(8,128)} %bitcast.18) | data formatting | bytes 131072
  44.4 1.3 %copy.15 = f32[8,128]{1,0:T(8,128)} copy(f32[8,128]{1,0:T(8,128)} %get-tuple-element.11) | data formatting | bytes 8192

commit v2 on v1

--- a/solution.py
+++ b/solution.py
@@ -93,8 +93,17 @@
     col_peers = [lax.rem(c + d, cols) for d in range(1, cols)]
     plane_peers = [a * PLANE + lax.rem(b + d, PLANE) for d in range(1, PLANE)]
     layer_peers = [lax.rem(a + d, layers) * PLANE + b for d in range(1, layers)]
-    for peer in layer_peers + plane_peers:
+    for peer in plane_peers:
         greet(peer, c)
+
+    @pl.when(a < layers - 1)
+    def _():
+        greet(r + PLANE, c)
+
+    @pl.when(a > 0)
+    def _():
+        greet(r - PLANE, c)
+
     for peer in col_peers:
         greet(r, peer)
 
@@ -108,7 +117,8 @@
         for k in range(cols):
             greet(r - 1, k)
 
-    expected = (cols - 1) + (PLANE - 1) + (layers - 1)
+    expected = (cols - 1) + (PLANE - 1)
+    expected = expected + jnp.where(a < layers - 1, 1, 0) + jnp.where(a > 0, 1, 0)
     expected = expected + jnp.where(r < rows - 1, cols, 0) + jnp.where(r > 0, cols, 0)
     pl.semaphore_wait(barrier, expected)
 
@@ -116,23 +126,38 @@
         return owner if h == 0 else tiles - 1 - owner
 
     send_at = [0]
-
-    def z_push(src, owner, h, row):
+    guarded = []
+
+    def z_push(src, owner, h, row, cond=None):
         j = tile_of(owner, h)
-        push(src, zbuf.at[j], z_send.at[send_at[0]], z_recv.at[j], row, c)
+        copy = remote(src, zbuf.at[j], z_send.at[send_at[0]], z_recv.at[j], row, c)
         send_at[0] += 1
-
-    def z_wait(owner, h):
+        if cond is None:
+            copy.start()
+            pending.append(copy)
+        else:
+            guarded.append((cond, copy))
+            pl.when(cond)(copy.start)
+
+    def z_wait(owner, h, cond=None):
         j = tile_of(owner, h)
-        remote(zbuf.at[j], zbuf.at[j], z_send.at[0], z_recv.at[j], r, c).wait_recv()
+        copy = remote(zbuf.at[j], zbuf.at[j], z_send.at[0], z_recv.at[j], r, c)
+        if cond is None:
+            copy.wait_recv()
+        else:
+            pl.when(cond)(copy.wait_recv)
 
     row_x = r + x_step
     row_y = r + y_step
     near = (row_y, row_x)
     far = (row_x, row_y)
-    for peer in layer_peers:
-        for h in range(2):
-            z_push(z_ref.at[h], r, h, peer)
+    row_up = jnp.minimum(r + PLANE, rows - PLANE + b)
+    row_down = jnp.maximum(r - PLANE, b)
+    can_up = a < layers - 1
+    can_down = a > 0
+    z_push(z_ref.at[0], r, 0, row_down, can_down)
+    z_push(z_ref.at[0], r, 0, row_up, can_up)
+    z_push(z_ref.at[1], r, 1, row_down, can_down)
     for h in range(2):
         z_push(z_ref.at[h], r, h, near[h])
         z_push(z_ref.at[h], r, h, far[h])
@@ -178,33 +203,37 @@
                 work.pop(0)()
 
     some(strips)
-    layer_owner = [lax.rem(a + d, layers) * PLANE + b for d in range(1, layers)]
-    for owner in layer_owner:
-        for h in range(2):
-            z_wait(owner, h)
+    offsets = []
+    for d in range(1, layers):
+        offsets += [(d, a + d < layers, jnp.minimum(a + d, layers - 1) * PLANE + b, (0, 1))]
+        offsets += [(-d, a - d >= 0, jnp.maximum(a - d, 0) * PLANE + b, (0,))]
+    for d, there, owner, kinds in offsets:
+        for h in kinds:
             j = tile_of(owner, h)
-            z_push(zbuf.at[j], owner, h, near[h])
-            z_push(zbuf.at[j], owner, h, far[h])
+            z_wait(owner, h, there)
+            z_push(zbuf.at[j], owner, h, row_down if d > 0 else row_up, there & (can_down if d > 0 else can_up))
+            z_push(zbuf.at[j], owner, h, near[h], there)
+            z_push(zbuf.at[j], owner, h, far[h], there)
         some(1)
     some(len(work))
     for i, peer in enumerate(col_peers):
         remote(z_ref, zpeer.at[peer], zp_send.at[i], zp_recv.at[peer], r, peer).wait_recv()
     second_step = (y_step, x_step)
-    for owner in [r] + layer_owner:
-        for h in range(2):
+    for d, there, owner, kinds in [(0, None, r, (0, 1))] + offsets:
+        for h in kinds:
             from_near = owner + second_step[h]
-            z_wait(from_near, h)
+            z_wait(from_near, h, there)
             j = tile_of(from_near, h)
-            z_push(zbuf.at[j], from_near, h, far[h])
+            z_push(zbuf.at[j], from_near, h, far[h], there)
         if spare:
             spare.pop(0)()
     while spare:
         spare.pop(0)()
     last_step = (x_step, y_step)
-    for owner in [r] + layer_owner:
-        for h in range(2):
-            z_wait(owner + last_step[h], h)
-            z_wait(owner + x_step + y_step, h)
+    for d, there, owner, kinds in [(0, None, r, (0, 1))] + offsets:
+        for h in kinds:
+            z_wait(owner + last_step[h], h, there)
+            z_wait(owner + x_step + y_step, h, there)
 
     group = 256 // rank
     lane_slot = lax.div(lax.broadcasted_iota(jnp.int32, (count, group * rank), 1), rank)
@@ -293,13 +322,13 @@
         two = [split(second_ref, at) for at in ats]
         got_one = [jnp.zeros((count, LANES), jnp.float32) for _ in ats]
         got_two = [jnp.zeros((count, LANES), jnp.float32) for _ in ats]
-        for h in range(2):
-            for j in range(tile // LANES):
-                entry = table(full, h, j)
-                number = own_first + h * (tile // LANES) + j
-                for i in range(batch):
-                    got_one[i] = jnp.where(one[i][0] == number, pick(entry, one[i][1]), got_one[i])
-                    got_two[i] = jnp.where(two[i][0] == number, pick(entry, two[i][1]), got_two[i])
+        for got, index in ((got_one, one), (got_two, two)):
+            for i in range(batch):
+                for h in range(2):
+                    for j in range(tile // LANES):
+                        entry = table(full, h, j)
+                        number = own_first + h * (tile // LANES) + j
+                        got[i] = jnp.where(index[i][0] == number, pick(entry, index[i][1]), got[i])
         for i in range(batch):
             diff[ats[i]] = got_one[i] - got_two[i]
         return carry
@@ -322,11 +351,11 @@
         ats = [step * batch + i for i in range(batch)]
         two = [split(second_ref, at) for at in ats]
         got = [jnp.zeros((count, LANES), jnp.float32) for _ in ats]
-        for h in range(2):
-            for j in range(tile // LANES):
-                entry = table(prev32, h, j)
-                number = h * (tile // LANES) + j
-                for i in range(batch):
+        for i in range(batch):
+            for h in range(2):
+                for j in range(tile // LANES):
+                    entry = table(prev32, h, j)
+                    number = h * (tile // LANES) + j
                     got[i] = jnp.where(two[i][0] == number, pick(entry, two[i][1]), got[i])
         for i in range(batch):
             differ = diff[ats[i]] - got[i]
@@ -366,6 +395,8 @@
 
     for copy in pending:
         copy.wait_send()
+    for cond, copy in guarded:
+        pl.when(cond)(copy.wait_send)
 
     @pl.when(r < rows - 1)
     def _():
@@ -419,7 +450,7 @@
             pltpu.VMEM((PLANE, 2 * count, NBIN), f32),
             pltpu.VMEM((layers, 2 * count, NBIN), f32),
             dma(2, shard // strip), dma(2, off), dma(v_parts), dma(v_parts),
-            dma(2 * (layers - 1) + 6 * layers + 8), dma(tiles), dma(off), dma(cols),
+            dma(16 * layers), dma(tiles), dma(off), dma(cols),
             dma(off), dma(cols), dma(off), dma(cols), dma(cols), dma(cols),
             dma(off), dma(cols), dma(PLANE), dma(PLANE), dma(layers), dma(layers),
         ],

time: 46 us -> 43.8 us (0.952)
  Pallas kernels: 40.8 us -> 38.6 us
    pallas_call x1, Pallas kernels: 40.8 us -> 38.6 us  [body(): pl.pallas_call(functools.partial(kernel, (rows, cols, count, shard, tile,...]
where the time goes in v2:
time: 43.8 us; the launch traced here: 43.4 us
  Pallas kernels  38.6 us (88%)
  local copies, waits for them, and re-layouts  4.19 us (10%)
  between operations  0.64 us (1%)
    pallas_call x1, Pallas kernels, body(): pl.pallas_call(functools.partial(kernel, (rows, cols, count, shard, tile,...  38.6 us
    unnamed x3, local copies, waits for them, and re-layouts  4.19 us

profile of v2, /device:TPU:0, one launch (start us, length us, event | category | flops | bytes accessed | tf_op | source)
XLA Modules:
  0.0 43.4 jit_solution(17513283152568148052)
XLA Ops:
  0.6 1.4 %copy.13 = bf16[8,2,1,1024]{3,0,1,2:T(8,128)(2,1)} copy(bf16[8,2,1,1024]{3,1,2,0:T(2,128)(2,1)} %param.8) | data formatting | bytes 65536 | tf_op args[0]
  2.0 38.6 %shard_map.95 = (f32[2,8,1024]{2,1,0:T(8,128)}, f32[8,128]{1,0:T(8,128)}) custom-call(bf16[2,8,1024]{2,1,0:T(8,128)(2,1)} %bitcast.17, bf16[2,1024,2048]{2,1,0:T(8,128)(2,1)} %bitcast.14, bf16[2048,1024]{1,0:T(8,128)(2,1)} %bitcast.15, bf16[2048,1024]{1,0:T(8,128)(2,1)} %bitcast.16, s32[1,32]{1,0:T(1,128)} %ranks_ref.1, s32[32,128]{1,0:T(8,128)} %bitcast.19, ...), custom_call_target="tpu_custom_call" | custom-call | tf_op jit(solution)/shard_map/pallas_call | solution.py:427
  40.6 1.5 %copy.11 = f32[8,2,1,1024]{3,2,1,0:T(1,128)} copy(f32[8,2,1,1024]{3,0,1,2:T(8,128)} %bitcast.18) | data formatting | bytes 131072
  42.2 1.3 %copy.15 = f32[8,128]{1,0:T(8,128)} copy(f32[8,128]{1,0:T(8,128)} %get-tuple-element.11) | data formatting | bytes 8192

commit v3 on v2

--- a/solution.py
+++ b/solution.py
@@ -16,12 +16,12 @@
 
 def kernel(
     dims,
-    z_ref, diag_ref, left_ref, right_ref, ranks_ref, first_ref, second_ref, bins_ref,
+    noise_ref, diag_ref, left_ref, right_ref, ranks_ref, first_ref, second_ref, bins_ref,
     samples_ref, vario_ref,
-    zbuf, zpeer, down, doff, vbuf, ubuf, proj, acc, full, sbf, prev, prev32, diff, red1, red2, red3,
+    z_ref, zbuf, zpeer, down, doff, vbuf, ubuf, proj, acc, full, sbf, prev, prev32, diff, red1, red3,
     own_sem, off_sem, v_sem, u_sem,
     z_send, z_recv, zp_send, zp_recv, pj_send, pj_recv, sm_send, sm_recv, pv_send, pv_recv,
-    r1_send, r1_recv, r2_send, r2_recv, r3_send, r3_recv,
+    r1_send, r1_recv, r3_send, r3_recv,
 ):
     rows, cols, count, shard, tile, rank, strip = dims
     layers = rows // PLANE
@@ -85,16 +85,21 @@
     for copy in v_copies + u_copies:
         copy.start()
 
+    for h in range(2):
+        z_ref[h] = noise_ref[...].astype(jnp.float32)[:, h].astype(jnp.bfloat16)
+
     barrier = pltpu.get_barrier_semaphore()
 
     def greet(row, col):
         pl.semaphore_signal(barrier, inc=1, device_id=(row, col), device_id_type=MESH)
 
     col_peers = [lax.rem(c + d, cols) for d in range(1, cols)]
-    plane_peers = [a * PLANE + lax.rem(b + d, PLANE) for d in range(1, PLANE)]
+    place = b * cols + c
+    block_slots = [lax.rem(place + d, PLANE * cols) for d in range(1, PLANE * cols)]
+    block_peers = [(a * PLANE + lax.div(m, cols), lax.rem(m, cols), m) for m in block_slots]
     layer_peers = [lax.rem(a + d, layers) * PLANE + b for d in range(1, layers)]
-    for peer in plane_peers:
-        greet(peer, c)
+    for row, col, slot in block_peers:
+        greet(row, col)
 
     @pl.when(a < layers - 1)
     def _():
@@ -103,9 +108,6 @@
     @pl.when(a > 0)
     def _():
         greet(r - PLANE, c)
-
-    for peer in col_peers:
-        greet(r, peer)
 
     @pl.when(r < rows - 1)
     def _():
@@ -117,7 +119,7 @@
         for k in range(cols):
             greet(r - 1, k)
 
-    expected = (cols - 1) + (PLANE - 1)
+    expected = PLANE * cols - 1
     expected = expected + jnp.where(a < layers - 1, 1, 0) + jnp.where(a > 0, 1, 0)
     expected = expected + jnp.where(r < rows - 1, cols, 0) + jnp.where(r > 0, cols, 0)
     pl.semaphore_wait(barrier, expected)
@@ -297,10 +299,7 @@
             copy.start()
 
     for h in range(2):
-        samples_ref[h] = value[h * count : (h + 1) * count]
-    for i, peer in enumerate(col_peers):
-        remote(full.at[c], full.at[peer], sm_send.at[i], sm_recv.at[peer], r, peer).wait_recv()
-
+        samples_ref[:, h, 0, :] = value[h * count : (h + 1) * count]
     groups = first_ref.shape[0]
     per_row = shard // LANES
     own_first = 2 * tile // LANES
@@ -316,24 +315,29 @@
     def pick(entry, low):
         return jnp.take_along_axis(entry, low, axis=1, mode="promise_in_bounds")
 
-    def own_part(step, carry):
+    def own_part(k, fresh, step, carry):
         ats = [step * batch + i for i in range(batch)]
-        one = [split(first_ref, at) for at in ats]
-        two = [split(second_ref, at) for at in ats]
-        got_one = [jnp.zeros((count, LANES), jnp.float32) for _ in ats]
-        got_two = [jnp.zeros((count, LANES), jnp.float32) for _ in ats]
-        for got, index in ((got_one, one), (got_two, two)):
-            for i in range(batch):
+        base = own_first + k * per_row
+        got = [[], []]
+        for which, ref in enumerate((first_ref, second_ref)):
+            for at in ats:
+                high, low = split(ref, at)
+                high = high - base
+                value = jnp.zeros((count, LANES), jnp.float32)
                 for h in range(2):
-                    for j in range(tile // LANES):
-                        entry = table(full, h, j)
-                        number = own_first + h * (tile // LANES) + j
-                        got[i] = jnp.where(index[i][0] == number, pick(entry, index[i][1]), got[i])
+                    for j in range(per_row):
+                        entry = full[k, h * count : (h + 1) * count, j * LANES : (j + 1) * LANES]
+                        value = jnp.where(high == h * (tile // LANES) + j, pick(entry, low), value)
+                got[which].append(value)
         for i in range(batch):
-            diff[ats[i]] = got_one[i] - got_two[i]
+            value = got[0][i] - got[1][i]
+            diff[ats[i]] = value if fresh else diff[ats[i]] + value
         return carry
 
-    lax.fori_loop(0, groups // batch, own_part, 0)
+    lax.fori_loop(0, groups // batch, functools.partial(own_part, c, True), 0)
+    for i, peer in enumerate(col_peers):
+        remote(full.at[c], full.at[peer], sm_send.at[i], sm_recv.at[peer], r, peer).wait_recv()
+        lax.fori_loop(0, groups // batch, functools.partial(own_part, peer, False), 0)
 
     @pl.when(r > 0)
     def _():
@@ -384,10 +388,7 @@
             out = out + buf[i]
         return out
 
-    total = reduce_stage(total, red1, c, [(r, p, p) for p in col_peers], r1_send, r1_recv, cols)
-    total = reduce_stage(
-        total, red2, b, [(p, c, lax.rem(p, PLANE)) for p in plane_peers], r2_send, r2_recv, PLANE
-    )
+    total = reduce_stage(total, red1, place, block_peers, r1_send, r1_recv, PLANE * cols)
     total = reduce_stage(
         total, red3, a, [(p, c, lax.div(p, PLANE)) for p in layer_peers], r3_send, r3_recv, layers
     )
@@ -417,7 +418,6 @@
     strip = min(256, shard)
     layers = rows // PLANE
     v_parts = 4
-    z = jnp.transpose(noise[:, :, 0], (1, 0, 2))
     dma = lambda *shape: pltpu.SemaphoreType.DMA(shape)
     vmem = pl.BlockSpec(memory_space=pltpu.VMEM)
     hbm = pl.BlockSpec(memory_space=pl.ANY)
@@ -427,12 +427,13 @@
     samples, vario = pl.pallas_call(
         functools.partial(kernel, (rows, cols, count, shard, tile, rank, strip)),
         out_shape=(
-            jax.ShapeDtypeStruct((2, count, shard), f32),
+            jax.ShapeDtypeStruct((count, 2, 1, shard), f32),
             jax.ShapeDtypeStruct((count, NBIN), f32),
         ),
         in_specs=[vmem, hbm, hbm, hbm, smem, vmem, vmem, vmem],
         out_specs=(vmem, vmem),
         scratch_shapes=[
+            pltpu.VMEM((2, count, shard), bf16),
             pltpu.VMEM((tiles, count, shard), bf16),
             pltpu.VMEM((cols, 2, count, shard), bf16),
             pltpu.VMEM((2, shard, shard), bf16),
@@ -446,17 +447,16 @@
             pltpu.VMEM((cols, 2 * count, shard), bf16),
             pltpu.VMEM((cols, 2 * count, shard), f32),
             pltpu.VMEM((pair_first.shape[2] // LANES, count, LANES), f32),
-            pltpu.VMEM((cols, 2 * count, NBIN), f32),
-            pltpu.VMEM((PLANE, 2 * count, NBIN), f32),
+            pltpu.VMEM((PLANE * cols, 2 * count, NBIN), f32),
             pltpu.VMEM((layers, 2 * count, NBIN), f32),
             dma(2, shard // strip), dma(2, off), dma(v_parts), dma(v_parts),
             dma(16 * layers), dma(tiles), dma(off), dma(cols),
             dma(off), dma(cols), dma(off), dma(cols), dma(cols), dma(cols),
-            dma(off), dma(cols), dma(PLANE), dma(PLANE), dma(layers), dma(layers),
+            dma(PLANE * cols), dma(PLANE * cols), dma(layers), dma(layers),
         ],
         compiler_params=pltpu.CompilerParams(collective_id=0, has_side_effects=True),
     )(
-        z,
+        noise.reshape(count, 2, shard),
         diag_factor.reshape(2, shard, tile),
         left_factor.reshape(tiles * rank, shard),
         right_factor.reshape(tiles * rank, shard),
@@ -465,7 +465,7 @@
         pair_partner.reshape(-1, LANES),
         bin_ids.reshape(-1, LANES),
     )
-    return jnp.transpose(samples, (1, 0, 2))[:, :, None, :], vario
+    return samples, vario
 
 
 def solution(mesh):

time: 43.8 us -> 41.7 us (0.952)
  local copies, waits for them, and re-layouts: 4.19 us -> 2.74 us
  Pallas kernels: 38.6 us -> 38.1 us
    unnamed x3 -> x2, local copies, waits for them, and re-layouts: 4.19 us -> 2.74 us
    pallas_call x1, Pallas kernels: 38.6 us -> 38.1 us  [body(): pl.pallas_call(functools.partial(kernel, (rows, cols, count, shard, tile,...]
where the time goes in v3:
time: 41.7 us; the launch traced here: 41.4 us
  Pallas kernels  38.1 us (91%)
  local copies, waits for them, and re-layouts  2.74 us (7%)
  between operations  0.64 us (2%)
    pallas_call x1, Pallas kernels, body(): pl.pallas_call(functools.partial(kernel, (rows, cols, count, shard, tile,...  38.1 us
    unnamed x2, local copies, waits for them, and re-layouts  2.74 us

profile of v3, /device:TPU:0, one launch (start us, length us, event | category | flops | bytes accessed | tf_op | source)
XLA Modules:
  0.0 41.4 jit_solution(2911128357411082948)
XLA Ops:
  0.6 38.1 %shard_map.95 = (f32[8,2,1,1024]{3,2,1,0:T(1,128)}, f32[8,128]{1,0:T(8,128)}) custom-call(bf16[8,2,1024]{2,1,0:T(2,128)(2,1)} %bitcast.10, bf16[2,1024,2048]{2,1,0:T(8,128)(2,1)} %bitcast.7, bf16[2048,1024]{1,0:T(8,128)(2,1)} %bitcast.8, bf16[2048,1024]{1,0:T(8,128)(2,1)} %bitcast.9, s32[1,32]{1,0:T(1,128)} %ranks_ref.1, s32[32,128]{1,0:T(8,128)} %bitcast.11, ...), custom_call_target="tpu_custom_call" | custom-call | tf_op jit(solution)/shard_map/pallas_call | solution.py:427
  38.7 1.5 %copy.12 = f32[8,2,1,1024]{3,2,1,0:T(1,128)} copy(f32[8,2,1,1024]{3,2,1,0:T(1,128)} %get-tuple-element.4) | data formatting | bytes 131072
  40.2 1.3 %copy.13 = f32[8,128]{1,0:T(8,128)} copy(f32[8,128]{1,0:T(8,128)} %get-tuple-element.5) | data formatting | bytes 8192

commit v4 on v3

--- a/solution.py
+++ b/solution.py
@@ -101,13 +101,8 @@
     for row, col, slot in block_peers:
         greet(row, col)
 
-    @pl.when(a < layers - 1)
-    def _():
-        greet(r + PLANE, c)
-
-    @pl.when(a > 0)
-    def _():
-        greet(r - PLANE, c)
+    for peer in layer_peers:
+        greet(peer, c)
 
     @pl.when(r < rows - 1)
     def _():
@@ -119,8 +114,7 @@
         for k in range(cols):
             greet(r - 1, k)
 
-    expected = PLANE * cols - 1
-    expected = expected + jnp.where(a < layers - 1, 1, 0) + jnp.where(a > 0, 1, 0)
+    expected = PLANE * cols - 1 + layers - 1
     expected = expected + jnp.where(r < rows - 1, cols, 0) + jnp.where(r > 0, cols, 0)
     pl.semaphore_wait(barrier, expected)
 
@@ -153,13 +147,13 @@
     row_y = r + y_step
     near = (row_y, row_x)
     far = (row_x, row_y)
-    row_up = jnp.minimum(r + PLANE, rows - PLANE + b)
-    row_down = jnp.maximum(r - PLANE, b)
-    can_up = a < layers - 1
-    can_down = a > 0
-    z_push(z_ref.at[0], r, 0, row_down, can_down)
-    z_push(z_ref.at[0], r, 0, row_up, can_up)
-    z_push(z_ref.at[1], r, 1, row_down, can_down)
+    others = []
+    for d in range(1, layers):
+        other = lax.rem(a + jnp.where(2 * a < layers, d, layers - d), layers)
+        others.append((other, other * PLANE + b))
+    for other, peer in others:
+        z_push(z_ref.at[0], r, 0, peer)
+        z_push(z_ref.at[1], r, 1, peer, other < a)
     for h in range(2):
         z_push(z_ref.at[h], r, h, near[h])
         z_push(z_ref.at[h], r, h, far[h])
@@ -204,38 +198,34 @@
             if work:
                 work.pop(0)()
 
-    some(strips)
-    offsets = []
-    for d in range(1, layers):
-        offsets += [(d, a + d < layers, jnp.minimum(a + d, layers - 1) * PLANE + b, (0, 1))]
-        offsets += [(-d, a - d >= 0, jnp.maximum(a - d, 0) * PLANE + b, (0,))]
-    for d, there, owner, kinds in offsets:
-        for h in kinds:
+    some(2)
+    offsets = [(owner, (None, other > a)) for other, owner in others]
+    for owner, there in offsets:
+        for h in range(2):
             j = tile_of(owner, h)
-            z_wait(owner, h, there)
-            z_push(zbuf.at[j], owner, h, row_down if d > 0 else row_up, there & (can_down if d > 0 else can_up))
-            z_push(zbuf.at[j], owner, h, near[h], there)
-            z_push(zbuf.at[j], owner, h, far[h], there)
+            z_wait(owner, h, there[h])
+            z_push(zbuf.at[j], owner, h, near[h], there[h])
+            z_push(zbuf.at[j], owner, h, far[h], there[h])
         some(1)
     some(len(work))
     for i, peer in enumerate(col_peers):
         remote(z_ref, zpeer.at[peer], zp_send.at[i], zp_recv.at[peer], r, peer).wait_recv()
     second_step = (y_step, x_step)
-    for d, there, owner, kinds in [(0, None, r, (0, 1))] + offsets:
-        for h in kinds:
+    for owner, there in [(r, (None, None))] + offsets:
+        for h in range(2):
             from_near = owner + second_step[h]
-            z_wait(from_near, h, there)
+            z_wait(from_near, h, there[h])
             j = tile_of(from_near, h)
-            z_push(zbuf.at[j], from_near, h, far[h], there)
+            z_push(zbuf.at[j], from_near, h, far[h], there[h])
         if spare:
             spare.pop(0)()
     while spare:
         spare.pop(0)()
     last_step = (x_step, y_step)
-    for d, there, owner, kinds in [(0, None, r, (0, 1))] + offsets:
-        for h in kinds:
-            z_wait(owner + last_step[h], h, there)
-            z_wait(owner + x_step + y_step, h, there)
+    for owner, there in [(r, (None, None))] + offsets:
+        for h in range(2):
+            z_wait(owner + last_step[h], h, there[h])
+            z_wait(owner + x_step + y_step, h, there[h])
 
     group = 256 // rank
     lane_slot = lax.div(lax.broadcasted_iota(jnp.int32, (count, group * rank), 1), rank)

time: 41.7 us -> 37.7 us (0.904)
  Pallas kernels: 38.1 us -> 34 us
    pallas_call x1, Pallas kernels: 38.1 us -> 34 us  [body(): pl.pallas_call(functools.partial(kernel, (rows, cols, count, shard, tile,...]
where the time goes in v4:
time: 37.7 us; the launch traced here: 37.4 us
  Pallas kernels  34 us (90%)
  local copies, waits for them, and re-layouts  2.74 us (7%)
  between operations  0.64 us (2%)
    pallas_call x1, Pallas kernels, body(): pl.pallas_call(functools.partial(kernel, (rows, cols, count, shard, tile,...  34 us
    unnamed x2, local copies, waits for them, and re-layouts  2.74 us

profile of v4, /device:TPU:0, one launch (start us, length us, event | category | flops | bytes accessed | tf_op | source)
XLA Modules:
  0.0 37.4 jit_solution(17058814358047792158)
XLA Ops:
  0.6 34.0 %shard_map.95 = (f32[8,2,1,1024]{3,2,1,0:T(1,128)}, f32[8,128]{1,0:T(8,128)}) custom-call(bf16[8,2,1024]{2,1,0:T(2,128)(2,1)} %bitcast.10, bf16[2,1024,2048]{2,1,0:T(8,128)(2,1)} %bitcast.7, bf16[2048,1024]{1,0:T(8,128)(2,1)} %bitcast.8, bf16[2048,1024]{1,0:T(8,128)(2,1)} %bitcast.9, s32[1,32]{1,0:T(1,128)} %ranks_ref.1, s32[32,128]{1,0:T(8,128)} %bitcast.11, ...), custom_call_target="tpu_custom_call" | custom-call | tf_op jit(solution)/shard_map/pallas_call | solution.py:417
  34.7 1.5 %copy.12 = f32[8,2,1,1024]{3,2,1,0:T(1,128)} copy(f32[8,2,1,1024]{3,2,1,0:T(1,128)} %get-tuple-element.4) | data formatting | bytes 131072
  36.1 1.3 %copy.13 = f32[8,128]{1,0:T(8,128)} copy(f32[8,128]{1,0:T(8,128)} %get-tuple-element.5) | data formatting | bytes 8192

commit v5 on v4

--- a/solution.py
+++ b/solution.py
@@ -207,9 +207,6 @@
             z_push(zbuf.at[j], owner, h, near[h], there[h])
             z_push(zbuf.at[j], owner, h, far[h], there[h])
         some(1)
-    some(len(work))
-    for i, peer in enumerate(col_peers):
-        remote(z_ref, zpeer.at[peer], zp_send.at[i], zp_recv.at[peer], r, peer).wait_recv()
     second_step = (y_step, x_step)
     for owner, there in [(r, (None, None))] + offsets:
         for h in range(2):
@@ -217,8 +214,10 @@
             z_wait(from_near, h, there[h])
             j = tile_of(from_near, h)
             z_push(zbuf.at[j], from_near, h, far[h], there[h])
-        if spare:
-            spare.pop(0)()
+        some(1)
+    some(len(work))
+    for i, peer in enumerate(col_peers):
+        remote(z_ref, zpeer.at[peer], zp_send.at[i], zp_recv.at[peer], r, peer).wait_recv()
     while spare:
         spare.pop(0)()
     last_step = (x_step, y_step)

time: 37.7 us -> 37.8 us (level)
  no operation moved by 1% of the time
where the time goes in v5:
time: 37.8 us; the launch traced here: 37.5 us
  Pallas kernels  34.1 us (90%)
  local copies, waits for them, and re-layouts  2.74 us (7%)
  between operations  0.64 us (2%)
    pallas_call x1, Pallas kernels, body(): pl.pallas_call(functools.partial(kernel, (rows, cols, count, shard, tile,...  34.1 us
    unnamed x2, local copies, waits for them, and re-layouts  2.74 us

profile of v5, /device:TPU:0, one launch (start us, length us, event | category | flops | bytes accessed | tf_op | source)
XLA Modules:
  0.0 37.5 jit_solution(10422790129524162777)
XLA Ops:
  0.6 34.1 %shard_map.95 = (f32[8,2,1,1024]{3,2,1,0:T(1,128)}, f32[8,128]{1,0:T(8,128)}) custom-call(bf16[8,2,1024]{2,1,0:T(2,128)(2,1)} %bitcast.10, bf16[2,1024,2048]{2,1,0:T(8,128)(2,1)} %bitcast.7, bf16[2048,1024]{1,0:T(8,128)(2,1)} %bitcast.8, bf16[2048,1024]{1,0:T(8,128)(2,1)} %bitcast.9, s32[1,32]{1,0:T(1,128)} %ranks_ref.1, s32[32,128]{1,0:T(8,128)} %bitcast.11, ...), custom_call_target="tpu_custom_call" | custom-call | tf_op jit(solution)/shard_map/pallas_call | solution.py:416
  34.8 1.5 %copy.12 = f32[8,2,1,1024]{3,2,1,0:T(1,128)} copy(f32[8,2,1,1024]{3,2,1,0:T(1,128)} %get-tuple-element.4) | data formatting | bytes 131072
  36.2 1.3 %copy.13 = f32[8,128]{1,0:T(8,128)} copy(f32[8,128]{1,0:T(8,128)} %get-tuple-element.5) | data formatting | bytes 8192
